TPU v7x, 256 devices: a whole 4x4x8 slice. The times are simulated.
256 devices in a mesh: build: 2 (over y_lo), test: 8 (over x, core), stmt: 16 (over y_hi, z).
Axes of the slice: x: 4, y: 4 (y_hi: 2, y_lo: 2; y = y_hi * 2 + y_lo), z: 8, core: 2. Of those that a mesh axis runs over, the one named last changes fastest.
Arguments:
- tile_values: bfloat16 [2, 8, 16, 2, 128, 128, 128], P('build', 'test', 'stmt'), may hold values from -6 to 6
- tile_test: int32 [2, 8, 16, 2], P('build', 'test', 'stmt'), may hold values from 0 to 3, as said below
- tile_stmt: int32 [2, 8, 16, 2], P('build', 'test', 'stmt'), may hold values from 0 to 1, as said below
- tile_build: int32 [2, 8, 16, 2], P('build', 'test', 'stmt'), may hold values from 0 to 5, as said below
- tile_count: int32 [2, 8, 16], P('build', 'test', 'stmt'), may hold values from 0 to 2, as said below
- test_factor: bfloat16 [8, 512, 256], P('test', ('build', 'stmt')), may hold values from -0.027063294 to 0.027063294
- build_factor: bfloat16 [2, 768, 256], P('build', ('test', 'stmt')), may hold values from -0.027063294 to 0.027063294
Outputs:
- stmt_factor: float32 [16, 256, 256], P('stmt', ('build', 'test'))
Inputs may be any that keep to these rules, and one draw needn't show every extreme that they name: `tile_count`: slots from this count on hold padding: their values and block numbers must not contribute. Some grid position has every slot live and some has none. `tile_test`: test block of a slot; the largest block is named in every draw. `tile_stmt`: statement block of a slot; the largest block is named in every draw. `tile_build`: build block of a slot; the largest block is named in every draw.
All inputs are finite; a program needn't handle non-finite values.
Results may differ from a plain program's by a relative error of at most 0.003.
Values may be sent and summed in bfloat16 or wider, within the bound.
A program may use at most 64 MiB of HBM per device.

v0:
```python
import jax
import jax.numpy as jnp
from jax import lax
from jax.sharding import PartitionSpec as P

TILE = 128
SB = 2
ALL = ("build", "test", "stmt")


def shards(tile_values, tile_test, tile_stmt, tile_build, tile_count, test_factor, build_factor):
    test_rows = test_factor[0]
    build_rows = build_factor[0]
    local_grams = jnp.stack(
        [
            lax.dot_general(
                test_rows, test_rows, (((0,), (0,)), ((), ())), preferred_element_type=jnp.float32
            ),
            lax.dot_general(
                build_rows, build_rows, (((0,), (0,)), ((), ())), preferred_element_type=jnp.float32
            ),
        ]
    )
    grams = lax.psum(local_grams, ALL)
    gram = grams[0] * grams[1]
    lower = jnp.linalg.cholesky(gram)
    test_slab = lax.all_gather(test_rows, ("build", "stmt"), axis=0, tiled=True)
    build_slab = lax.all_gather(build_rows, ("test", "stmt"), axis=0, tiled=True)
    slot_values = tile_values[0, 0, 0]
    slot_tests = tile_test[0, 0, 0]
    slot_stmts = tile_stmt[0, 0, 0]
    slot_builds = tile_build[0, 0, 0]
    live_count = tile_count[0, 0, 0]
    tile_width = slot_values.shape[-1]
    rank_width = test_slab.shape[1]
    running_sum = jnp.zeros((SB * TILE, rank_width), jnp.float32)
    for slot_index in range(slot_values.shape[0]):
        test_block = lax.dynamic_slice_in_dim(
            test_slab, slot_tests[slot_index] * tile_width, tile_width, 0
        ).astype(jnp.float32)
        build_block = lax.dynamic_slice_in_dim(
            build_slab, slot_builds[slot_index] * tile_width, tile_width, 0
        ).astype(jnp.float32)
        khatri_rao = (test_block[:, None, :] * build_block[None, :, :]).astype(jnp.bfloat16)
        term = jnp.einsum(
            "ijk,ikr->jr", slot_values[slot_index], khatri_rao, preferred_element_type=jnp.float32
        )
        live_weight = (slot_index < live_count).astype(jnp.float32)
        accumulate_term = term * live_weight
        start_row = slot_stmts[slot_index] * tile_width
        current = lax.dynamic_slice_in_dim(running_sum, start_row, tile_width, 0)
        running_sum = lax.dynamic_update_slice_in_dim(
            running_sum, current + accumulate_term, start_row, 0
        )
    owned_sums = lax.psum_scatter(running_sum, ("build", "test"), scatter_dimension=0, tiled=True)
    halfway = lax.linalg.triangular_solve(
        lower, owned_sums, left_side=False, lower=True, transpose_a=True
    )
    solved = lax.linalg.triangular_solve(
        lower, halfway, left_side=False, lower=True, transpose_a=False
    )
    return solved[None]


def solution(mesh):
    return jax.shard_map(
        shards,
        mesh=mesh,
        in_specs=(
            P("build", "test", "stmt", None, None, None, None),
            P("build", "test", "stmt", None),
            P("build", "test", "stmt", None),
            P("build", "test", "stmt", None),
            P("build", "test", "stmt"),
            P("test", ("build", "stmt"), None),
            P("build", ("test", "stmt"), None),
        ),
        out_specs=P("stmt", ("build", "test"), None),
        check_vma=False,
    )
```

profile of v0, /device:TPU:32, one launch (start us, length us, event | category | flops | bytes accessed | tf_op | source)
XLA Modules:
  0.0 509.7 jit_solution(10829243908084318337)
XLA Ops:
  7.4 0.0 all-reduce.3.cloned.1.call-start
  7.4 1.0 convolution_bitcast_fusion
  8.4 1.0 convolution_bitcast_fusion.1
  9.4 0.8 pad_maximum_fusion
  10.2 0.0 all-reduce.3.cloned.1.call-update
  10.2 0.0 reduce-scatter.2.cloned.1.call-start
  10.3 1.3 fusion.53
  12.9 0.7 copy.15
  13.6 1.3 fusion.52
  16.2 73.7 %all-gather = bf16[1,512,256]{2,1,0:T(8,128)(2,1)S(1)} all-gather(bf16[1,16,256]{2,1,0:T(8,128)(2,1)} %param.12), channel_id=2, replica_groups=mesh['build'=2,'test'=8,'stmt'=16] {'build','stmt'}, dimensions={1}, use_global_device_ids=true | all-gather | bytes 270336 | tf_op jit(solution)/shard_map/all_gather | solution.py:27
  89.9 1.3 fusion.54
  92.5 328.3 %all-gather.1 = bf16[1,768,256]{2,0,1:T(2,128)(2,1)S(1)} all-gather(bf16[1,6,256]{2,0,1:T(2,128)(2,1)S(1)} %copy.15), channel_id=3, replica_groups=mesh['build'=2,'test'=8,'stmt'=16] {'test','stmt'}, dimensions={1}, use_global_device_ids=true | all-gather | bytes 396288 | tf_op jit(solution)/shard_map/all_gather | solution.py:28
  420.8 0.3 dynamic-slice_convert_fusion
  421.1 0.1 copy.27
  421.8 0.1 copy.29
  422.0 0.0 slice-start
  422.0 0.0 slice-start.1
  422.0 9.1 %fusion.28 = f32[256,256]{1,0:T(8,128)S(1)} fusion(f32[256,256]{1,0:T(8,128)S(1)} %broadcast_in_dim.6, s32[]{:T(128)S(6)} %select_n.25, bf16[1,1,1,2,128,128,128]{6,5,4,3,2,1,0:T(8,128)(2,1)} %param.7, f32[128,256]{0,1:T(8,128)S(1)} %bitcast.119, f32[128,256]{1,0:T(8,128)S(1)} %get-tuple-element.26, f32[]{:T(128)} %bitcast.6), kind=kOutput, calls=%fused_computation.22 | convolution fusion | flops 1082163200 | bytes 4588036 | tf_op jit(solution)/shard_map/ijk,ikr->jr/dot_general | solution.py:45
  431.2 0.0 slice-done
  431.2 5.3 %fusion.34 = f32[256,256]{1,0:T(8,128)S(1)} fusion(f32[256,256]{1,0:T(8,128)S(1)} %fusion.28, s32[]{:T(128)S(6)} %select_n.26, bf16[1,1,1,2,128,128,128]{6,5,4,3,2,1,0:T(8,128)(2,1)S(1)} %bitcast.122, f32[128,256]{0,1:T(8,128)S(1)} %bitcast.120, f32[128,256]{1,0:T(8,128)S(1)} %get-tuple-element.25, f32[]{:T(128)} %bitcast.16), kind=kOutput, calls=%fused_computation.24 | convolution fusion | flops 1082195968 | bytes 4718600 | tf_op jit(solution)/shard_map/ijk,ikr->jr/dot_general | solution.py:45
  436.5 0.0 copy-start
  436.5 0.7 copy-done
  437.2 0.0 reduce-scatter.2.cloned.1.call-update
  437.2 0.0 all-reduce.3.cloned.1.call-done
  437.2 1.1 fusion.38
  438.3 0.1 copy.22
  438.4 1.1 fusion.37
  439.5 11.7 %cholesky.49 = f32[128,128]{1,0:T(8,128)S(1)} custom-call(f32[128,128]{1,0:T(8,128)S(1)} %cholesky.115), custom_call_target="Cholesky" | custom-call | tf_op jit(solution)/shard_map/jit(cholesky)/cholesky | solution.py:26
  451.3 9.8 %custom-call.16 = f32[1,128,128]{1,2,0:T(8,128)S(1)} custom-call(f32[1,128,128]{2,1,0:T(8,128)S(1)} %get-tuple-element.30), custom_call_target="InvertDiagBlocksLowerTriangular" | custom-call | tf_op jit(solution)/shard_map/jit(cholesky)/cholesky | solution.py:26
  461.1 0.2 constant_dynamic-update-slice_fusion
  461.3 0.3 convolution_subtract_fusion
  461.6 11.7 %cholesky.103 = f32[128,128]{1,0:T(8,128)S(1)} custom-call(f32[128,128]{1,0:T(8,128)S(1)} %convolution_subtract_fusion), custom_call_target="Cholesky" | custom-call | tf_op jit(solution)/shard_map/jit(cholesky)/cholesky | solution.py:26
  473.4 0.7 compare_reduce_fusion
  475.2 0.1 triangular_solve.67
  475.3 3.8 while.1
  475.3 0.6 fusion.63
  475.9 1.3 bitcast_dynamic-update-slice_fusion.2
  477.2 0.6 fusion.63
  477.8 1.3 bitcast_dynamic-update-slice_fusion.2
  479.1 19.9 %custom-call.17 = f32[2,128,128]{1,2,0:T(8,128)S(1)} custom-call(f32[2,128,128]{2,1,0:T(8,128)S(1)} %get-tuple-element.12), custom_call_target="InvertDiagBlocksLowerTriangular" | custom-call | tf_op jit(solution)/shard_map/triangular_solve | solution.py:56
  499.0 0.0 reduce-scatter.2.cloned.1.call-done
  499.0 0.8 fusion.43
  499.9 0.9 convolution_subtract_fusion.2
  500.8 0.2 fusion.45
  501.0 0.2 fusion.44
  501.2 0.2 convolution_subtract_fusion.1
  501.4 0.2 fusion.42
  501.6 0.7 maximum_bitcast_fusion
  (13 shorter events, 0.2 us)
Async XLA Ops:
  7.4 429.9 %all-reduce.3.cloned.1.call-start = ((), (), s32[]{:S(2)}) async-start(), calls=%async_computation.2 | async-start | bytes 1048576 | tf_op jit(solution)/shard_map/psum | solution.py:24
  10.2 488.8 %reduce-scatter.2.cloned.1.call-start = ((), (), s32[]{:S(2)}) async-start(), calls=%async_computation.1 | async-start | bytes 278528 | tf_op jit(solution)/shard_map/reduce_scatter | solution.py:55
  422.0 9.2 %slice-start = ((s8[8388608]{0:T(1024)(128)(4,1)}), s8[4194304]{0:T(1024)(128)(4,1)S(1)}, s32[]{:S(2)}) async-start(s8[8388608]{0:T(1024)(128)(4,1)} %bitcast.121), calls=%async_computation.3 | async-start | bytes 8388608
  422.0 9.2 %slice-start.1 = ((s8[8388608]{0:T(1024)(128)(4,1)}), s8[4194304]{0:T(1024)(128)(4,1)S(1)}, s32[]{:S(2)}) async-start(s8[8388608]{0:T(1024)(128)(4,1)} %bitcast.121), calls=%async_computation.4 | async-start | bytes 8388608
  436.5 0.7 copy-start
Sparse Core Ops, SparseCore 0:
  13.6 256.4 all-reduce.2
Sparse Core Ops, SparseCore 1:
  437.3 56.1 reduce-scatter.1
where the time goes:
time: 510 us
  blocking collectives  402 us (79%)
  other arithmetic  57.8 us (11%)
  between operations  20.7 us (4%)
  matrix products  19.4 us (4%)
  local copies, waits for them, and re-layouts  9.57 us (2%)
    all_gather x1, blocking collectives, shards(): lax.all_gather(build_rows, ('test', 'stmt'), axis=0, tiled=True)  328 us
    all_gather x1, blocking collectives, shards(): test_slab = lax.all_gather(test_rows, ('build', 'stmt'), axis=0, tiled=True)  73.7 us
    another operation x6, other arithmetic, shards(): lower = jnp.linalg.cholesky(gram)  34 us
    another operation x3, other arithmetic, shards(): lax.linalg.triangular_solve(lower, owned_sums, left_side=False, lower=Tru...  19.9 us
    dot_general x2, matrix products, shards(): jnp.einsum('ijk,ikr->jr', slot_values[slot_index], khatri_rao, preferred_...  14.4 us
  transfers between devices with their start and end apart: 2, of which 0 were waited for; matrix products, arithmetic and copies ran while one was open for 16% of the time, Pallas kernels for 0%

commit v1 on v0

--- a/solution.py
+++ b/solution.py
@@ -1,3 +1,4 @@
+import functools
 import jax
 import jax.numpy as jnp
 from jax import lax
@@ -6,6 +7,16 @@
 TILE = 128
 SB = 2
 ALL = ("build", "test", "stmt")
+
+
+def load_kinds(frame, which_axis):
+    return jnp.concatenate(
+        jax.lax.all_to_all(jnp.stack([frame] * jax.lax.psum(1, which_axis)), which_axis, 0, 0),
+        axis=0,
+    )
+
+
+pack_ticks = functools.partial(load_kinds, which_axis=("test", "stmt"))
 
 
 def shards(tile_values, tile_test, tile_stmt, tile_build, tile_count, test_factor, build_factor):
@@ -25,7 +36,7 @@
     gram = grams[0] * grams[1]
     lower = jnp.linalg.cholesky(gram)
     test_slab = lax.all_gather(test_rows, ("build", "stmt"), axis=0, tiled=True)
-    build_slab = lax.all_gather(build_rows, ("test", "stmt"), axis=0, tiled=True)
+    build_slab = pack_ticks(build_rows)
     slot_values = tile_values[0, 0, 0]
     slot_tests = tile_test[0, 0, 0]
     slot_stmts = tile_stmt[0, 0, 0]

time: 510 us -> 403 us (0.79)
  blocking collectives: 402 us -> 71.5 us
  waiting for transfers between devices: 0.08 us -> 205 us
  starting transfers between devices: 0.05 us -> 15.1 us
    all_gather x1 -> x0, blocking collectives: 328 us -> none  [shards(): lax.all_gather(build_rows, ('test', 'stmt'), axis=0, tiled=True)]
    psum x1, waiting for transfers between devices: 0.02 us -> 164 us  [shards(): grams = lax.psum(local_grams, ALL)]
    reduce_scatter x1, waiting for transfers between devices: 0.03 us -> 41.1 us  [shards(): lax.psum_scatter(running_sum, ('build', 'test'), scatter_dimension=0, til...]
    all_to_all x0 -> x1, starting transfers between devices: none -> 15 us  [load_kinds(): jax.lax.all_to_all(jnp.stack([frame] * jax.lax.psum(1, which_axis)), whic...]
  transfers between devices with their start and end apart: 2 -> 3, of which waited for: 0 -> 2; matrix products, arithmetic and copies ran while one was open for 16% -> 16% of each run, Pallas kernels for 0% -> 0%
where the time goes in v1:
time: 403 us; the launch traced here: 402 us
  waiting for transfers between devices  205 us (51%)
  blocking collectives  71.5 us (18%)
  other arithmetic  57.4 us (14%)
  matrix products  21.8 us (5%)
  between operations  20.6 us (5%)
  starting transfers between devices  15.1 us (4%)
  local copies, waits for them, and re-layouts  10.9 us (3%)
    psum x1, waiting for transfers between devices, shards(): grams = lax.psum(local_grams, ALL)  164 us
    all_gather x1, blocking collectives, shards(): test_slab = lax.all_gather(test_rows, ('build', 'stmt'), axis=0, tiled=True)  71.5 us
    reduce_scatter x1, waiting for transfers between devices, shards(): lax.psum_scatter(running_sum, ('build', 'test'), scatter_dimension=0, til...  41.1 us
    another operation x6, other arithmetic, shards(): lower = jnp.linalg.cholesky(gram)  34 us
    another operation x3, other arithmetic, shards(): lax.linalg.triangular_solve(lower, owned_sums, left_side=False, lower=Tru...  19.7 us
    dot_general x2, matrix products, shards(): jnp.einsum('ijk,ikr->jr', slot_values[slot_index], khatri_rao, preferred_...  16.8 us
    all_to_all x1, starting transfers between devices, load_kinds(): jax.lax.all_to_all(jnp.stack([frame] * jax.lax.psum(1, which_axis)), whic...  15 us
  transfers between devices with their start and end apart: 3, of which 2 were waited for; matrix products, arithmetic and copies ran while one was open for 16% of the time, Pallas kernels for 0%

profile of v1, /device:TPU:32, one launch (start us, length us, event | category | flops | bytes accessed | tf_op | source)
XLA Modules:
  0.0 401.9 jit_solution(10253872871679277303)
XLA Ops:
  7.4 0.0 all-reduce.3.cloned.1.call-start
  7.4 1.0 convolution_bitcast_fusion
  8.4 1.0 convolution_bitcast_fusion.1
  9.4 0.8 pad_maximum_fusion
  10.2 0.0 all-reduce.3.cloned.1.call-update
  10.2 1.5 stack.12
  11.7 15.0 %all-to-all-start = ((bf16[128,6,256]{2,1,0:T(8,128)(2,1)}), bf16[128,6,256]{2,1,0:T(8,128)(2,1)S(1)}, u32[]{:S(2)}, u32[]{:S(2)}) async-start(bf16[128,6,256]{2,1,0:T(8,128)(2,1)} %stack.12), calls=%async_computation | async-start | bytes 1048576 | tf_op jit(solution)/shard_map/all_to_all | solution.py:14
  26.7 0.0 reduce-scatter.2.cloned.1.call-start
  26.8 1.4 fusion.53
  28.2 1.4 fusion.52
  29.6 1.4 fusion.54
  35.4 71.5 %all-gather = bf16[1,512,256]{2,1,0:T(8,128)(2,1)S(1)} all-gather(bf16[1,16,256]{2,1,0:T(8,128)(2,1)} %param.12), channel_id=2, replica_groups=mesh['build'=2,'test'=8,'stmt'=16] {'build','stmt'}, dimensions={1}, use_global_device_ids=true | all-gather | bytes 270336 | tf_op jit(solution)/shard_map/all_gather | solution.py:38
  106.9 163.6 %all-reduce.3.cloned.1.call-done = f32[2,256,256]{1,2,0:T(8,128)} async-done(((f32[2,256,256]{1,2,0:T(8,128)}), f32[2,256,256]{1,2,0:T(8,128)}) %all-reduce.3.cloned.1.call-update) | async-done | bytes 524304 | tf_op jit(solution)/shard_map/psum | solution.py:35
  270.5 1.1 fusion.38
  271.5 0.1 copy.20
  271.7 1.1 fusion.37
  272.8 11.7 %cholesky.49 = f32[128,128]{1,0:T(8,128)S(1)} custom-call(f32[128,128]{1,0:T(8,128)S(1)} %cholesky.115), custom_call_target="Cholesky" | custom-call | tf_op jit(solution)/shard_map/jit(cholesky)/cholesky | solution.py:37
  284.5 9.8 %custom-call.16 = f32[1,128,128]{1,2,0:T(8,128)S(1)} custom-call(f32[1,128,128]{2,1,0:T(8,128)S(1)} %get-tuple-element.30), custom_call_target="InvertDiagBlocksLowerTriangular" | custom-call | tf_op jit(solution)/shard_map/jit(cholesky)/cholesky | solution.py:37
  294.4 0.2 constant_dynamic-update-slice_fusion
  294.6 0.3 convolution_subtract_fusion
  294.9 11.7 %cholesky.103 = f32[128,128]{1,0:T(8,128)S(1)} custom-call(f32[128,128]{1,0:T(8,128)S(1)} %convolution_subtract_fusion), custom_call_target="Cholesky" | custom-call | tf_op jit(solution)/shard_map/jit(cholesky)/cholesky | solution.py:37
  306.6 0.7 compare_reduce_fusion
  308.5 0.0 all-to-all-done
  308.5 0.1 reshape.66
  308.7 0.1 copy.14
  308.8 0.1 copy.16
  308.9 8.5 %fusion.28 = f32[256,256]{1,0:T(8,128)S(1)} fusion(f32[256,256]{1,0:T(8,128)S(1)} %broadcast_in_dim.6, s32[]{:T(128)S(6)} %select_n.25, bf16[1,1,1,2,128,128,128]{6,5,4,3,2,1,0:T(8,128)(2,1)} %param.7, f32[128,256]{0,1:T(8,128)S(1)} %copy.14, f32[128,256]{1,0:T(8,128)S(1)} %get-tuple-element.26, f32[]{:T(128)} %bitcast.6), kind=kOutput, calls=%fused_computation.22 | convolution fusion | flops 1082163200 | bytes 4588036 | tf_op jit(solution)/shard_map/ijk,ikr->jr/dot_general | solution.py:56
  317.4 8.3 %fusion.34 = f32[256,256]{1,0:T(8,128)S(1)} fusion(f32[256,256]{1,0:T(8,128)S(1)} %fusion.28, s32[]{:T(128)S(6)} %select_n.26, bf16[1,1,1,2,128,128,128]{6,5,4,3,2,1,0:T(8,128)(2,1)} %param.7, f32[128,256]{0,1:T(8,128)S(1)} %copy.16, f32[128,256]{1,0:T(8,128)S(1)} %get-tuple-element.25, f32[]{:T(128)} %bitcast.15), kind=kOutput, calls=%fused_computation.24 | convolution fusion | flops 1082195968 | bytes 4719108 | tf_op jit(solution)/shard_map/ijk,ikr->jr/dot_general | solution.py:56
  325.7 0.0 copy-start
  325.7 0.7 copy-done
  326.4 0.0 reduce-scatter.2.cloned.1.call-update
  326.4 0.1 triangular_solve.67
  326.5 4.1 %while.1 = (s32[]{:T(128)}, f32[256,256]{1,0:T(8,128)S(1)}, s32[2,2]{1,0:T(2,128)S(1)}, f32[2,128,128]{2,1,0:T(8,128)S(1)}, s32[]{:T(128)}) while((s32[]{:T(128)}, f32[256,256]{1,0:T(8,128)S(1)}, s32[2,2]{1,0:T(2,128)S(1)}, f32[2,128,128]{2,1,0:T(8,128)S(1)}, s32[]{:T(128)}) %tuple.28), condition=%wide.while_cond, body=%wide.while_body.sunk | while | flops 2 | bytes 131181 | solution.py:67
  326.5 0.7 fusion.63
  327.2 1.3 bitcast_dynamic-update-slice_fusion.2
  328.5 0.7 fusion.63
  329.2 1.3 bitcast_dynamic-update-slice_fusion.2
  330.5 19.7 %custom-call.17 = f32[2,128,128]{1,2,0:T(8,128)S(1)} custom-call(f32[2,128,128]{2,1,0:T(8,128)S(1)} %get-tuple-element.12), custom_call_target="InvertDiagBlocksLowerTriangular" | custom-call | tf_op jit(solution)/shard_map/triangular_solve | solution.py:67
  350.2 41.1 %reduce-scatter.2.cloned.1.call-done = f32[16,256]{1,0:T(8,128)} async-done(((f32[256,256]{1,0:T(8,128)}), f32[16,256]{1,0:T(8,128)}) %reduce-scatter.2.cloned.1.call-update) | async-done | bytes 16400 | tf_op jit(solution)/shard_map/reduce_scatter | solution.py:66
  391.3 0.8 fusion.43
  392.1 0.9 convolution_subtract_fusion.2
  393.0 0.2 fusion.45
  393.2 0.2 fusion.44
  393.4 0.2 convolution_subtract_fusion.1
  393.6 0.2 fusion.42
  393.8 0.7 maximum_bitcast_fusion
  (12 shorter events, 0.2 us)
Async XLA Ops:
  7.4 263.1 %all-reduce.3.cloned.1.call-start = ((), (), s32[]{:S(2)}) async-start(), calls=%async_computation.3 | async-start | bytes 1048576 | tf_op jit(solution)/shard_map/psum | solution.py:35
  11.7 296.7 %all-to-all-start = ((bf16[128,6,256]{2,1,0:T(8,128)(2,1)}), bf16[128,6,256]{2,1,0:T(8,128)(2,1)S(1)}, u32[]{:S(2)}, u32[]{:S(2)}) async-start(bf16[128,6,256]{2,1,0:T(8,128)(2,1)} %stack.12), calls=%async_computation | async-start | bytes 1048576 | tf_op jit(solution)/shard_map/all_to_all | solution.py:14
  26.7 364.6 %reduce-scatter.2.cloned.1.call-start = ((), (), s32[]{:S(2)}) async-start(), calls=%async_computation.2 | async-start | bytes 278528 | tf_op jit(solution)/shard_map/reduce_scatter | solution.py:66
  325.7 0.7 copy-start
Sparse Core Ops, SparseCore 0:
  13.6 256.8 all-reduce.2
Sparse Core Ops, SparseCore 1:
  326.5 64.7 reduce-scatter.1
